TPU v7x, 32 devices: a whole 2x2x4 slice. The times are simulated.
32 devices in a mesh: grp: 2 (over x), filt: 8 (over z, y), sky: 2 (over core).
Axes of the slice: x: 2, y: 2, z: 4, core: 2. Of those that a mesh axis runs over, the one named last changes fastest.
Arguments:
- strain: bfloat16 [2, 6, 524288], P(None, 'grp', 'filt'), parts along dimension 1, may hold values from -4 to 4
- templates: bfloat16 [2, 4, 524288], P(None, 'sky', 'filt'), may hold values from -6 to 6
- lengths: int32 [4], P('sky'), may hold values from 131072 to 524288
- antenna: bfloat16 [2, 3, 3072], P(None, None, 'sky'), may hold values from -1 to 1
- delays: int32 [3, 3072], P(None, 'sky'), may hold values from -48 to 48
Outputs:
- peak: float32 [2, 2048, 3072], P('grp', 'filt', 'sky'), parts along dimension 0
There are 2 independent parts, one for each index of `grp`. A program takes and returns all parts, laid end to end along the dimension named above; an argument that names none is the same for every part. Nothing has to cross between parts.
All inputs are finite; a program needn't handle non-finite values.
Results may differ from a plain program's by a relative error of at most 0.018.
Values may be sent and summed in bfloat16 or wider, within the bound.
A program may use at most 64 MiB of HBM per device.

v0:
```python
import functools

import jax
import jax.numpy as jnp
import numpy as np
from jax import lax
from jax.experimental import pallas as pl
from jax.experimental.pallas import tpu as pltpu
from jax.sharding import PartitionSpec as P

N1 = 2048
N2 = 512
DM = 48
NF = N1 * N2
LANE = 128
FINE = 16
TWO_PI = 2.0 * np.pi
CENTRE = N1 - DM + N1 // 2
MESH = pl.DeviceIdType.MESH
F32 = jnp.float32
BF16 = jnp.bfloat16


def host_table(rows, step, columns, period):
    phase = (np.arange(rows)[:, None] * step * columns[None, :]) % period
    angle = phase * (TWO_PI / period)
    return jnp.asarray(np.stack([np.cos(angle), np.sin(angle)]).astype(np.float32))


def outer_turn(coarse, fine):
    c_re, c_im = coarse[0], coarse[1]
    f_re, f_im = fine[0], fine[1]
    re, im = [], []
    for row in range(c_re.shape[0]):
        u, v = c_re[row : row + 1], c_im[row : row + 1]
        re.append(u * f_re - v * f_im)
        im.append(u * f_im + v * f_re)
    return jnp.concatenate(re, axis=0), jnp.concatenate(im, axis=0)


def transform_kernel(
    limits, s_ref, h_ref, pa_ref, pb_ref, bc_ref, bf_ref, ac_ref, af_ref, z_ref, x_ref, zs_ref, nrm_ref
):
    step = pl.program_id(0)
    blocks = pl.num_programs(0)
    temps, rows = h_ref.shape[1], h_ref.shape[2]
    dets = s_ref.shape[1]

    @pl.when(step == 0)
    def _():
        p_re, p_im = outer_full(pa_ref, pb_ref)
        ids = lax.broadcasted_iota(jnp.int32, (rows, N2), 0) * N2 + lax.broadcasted_iota(
            jnp.int32, (rows, N2), 1
        )
        for k in range(temps):
            keep = ids < limits[k]
            h_re = jnp.where(keep, h_ref[0, k].astype(F32), 0.0)
            h_im = jnp.where(keep, h_ref[1, k].astype(F32), 0.0)
            norm = jnp.sum(h_re * h_re + h_im * h_im, axis=0, keepdims=True)
            norm = jnp.broadcast_to(jnp.sum(norm, axis=1, keepdims=True), (1, LANE))
            high = norm.astype(BF16).astype(F32)
            nrm_ref[2 * k : 2 * k + 1] = high
            nrm_ref[2 * k + 1 : 2 * k + 2] = norm - high
            g_re = h_re * p_re + h_im * p_im
            g_im = h_re * p_im - h_im * p_re
            for d in range(dets):
                s_re = s_ref[0, d].astype(F32)
                s_im = s_ref[1, d].astype(F32)
                start = (k * dets + d) * 2 * rows
                x_ref[start : start + rows] = (g_re * s_re - g_im * s_im).astype(BF16)
                x_ref[start + rows : start + 2 * rows] = (g_re * s_im + g_im * s_re).astype(BF16)

    t_re, t_im = outer_turn(bc_ref[...], bf_ref[...])
    table = jnp.concatenate([t_re.astype(BF16), t_im.astype(BF16)], axis=1)
    a_re, a_im = outer_turn(ac_ref[...], af_ref[...])
    for item in range(temps * dets):
        start = item * 2 * rows
        r = jnp.dot(x_ref[start : start + 2 * rows], table, preferred_element_type=F32)
        c_re, s_re = r[:rows, :LANE], r[:rows, LANE:]
        c_im, s_im = r[rows:, :LANE], r[rows:, LANE:]
        u_re = jnp.sum(a_re * c_re - a_im * s_re, axis=0, keepdims=True)
        u_im = jnp.sum(a_re * c_im - a_im * s_im, axis=0, keepdims=True)
        v_re = jnp.sum(a_re * s_re + a_im * c_re, axis=0, keepdims=True)
        v_im = jnp.sum(a_re * s_im + a_im * c_im, axis=0, keepdims=True)
        zs_ref[0, 2 * item : 2 * item + 1] = u_re - v_im
        zs_ref[0, 2 * item + 1 : 2 * item + 2] = u_im + v_re
        zs_ref[1, 2 * item : 2 * item + 1] = u_re + v_im
        zs_ref[1, 2 * item + 1 : 2 * item + 2] = u_im - v_re
    tail = 2 * temps * dets
    zs_ref[0, tail : tail + 2 * temps] = nrm_ref[...]
    zs_ref[1, tail : tail + 2 * temps] = nrm_ref[...]
    flip = (
        lax.broadcasted_iota(jnp.int32, (LANE, LANE), 0)
        + lax.broadcasted_iota(jnp.int32, (LANE, LANE), 1)
        == LANE - 1
    )
    flip = jnp.where(flip, 1.0, 0.0).astype(BF16)
    ahead = jnp.dot(zs_ref[0].astype(BF16), flip, preferred_element_type=F32)
    z_ref[blocks - 1 - step] = ahead.astype(BF16)
    z_ref[blocks + step] = zs_ref[1].astype(BF16)


def outer_full(pa_ref, pb_ref):
    a_re, a_im = pa_ref[0], pa_ref[1]
    b_re, b_im = pb_ref[0], pb_ref[1]
    return a_re * b_re - a_im * b_im, a_re * b_im + a_im * b_re


def exchange_kernel(devices, skies, first, own, z_ref, got_ref, send_sem, recv_sem, local_sem):
    me = lax.axis_index("filt")
    side = lax.axis_index("sky")
    count = got_ref.shape[2]
    barrier = pltpu.get_barrier_semaphore()
    peers = [(o, q) for q in range(skies) for o in range(devices) if (o, q) != (0, 0)]
    for o, q in peers:
        pl.semaphore_signal(
            barrier,
            inc=1,
            device_id={"filt": lax.rem(me + o, devices), "sky": lax.rem(side + q, skies)},
            device_id_type=MESH,
        )
    pl.semaphore_wait(barrier, len(peers))

    def piece(target):
        return z_ref.at[pl.ds((first - own * target) // LANE, count)]

    mine = pltpu.make_async_copy(piece(me), got_ref.at[side, me], local_sem)
    mine.start()
    copies = []
    for n, (o, q) in enumerate(peers):
        target = lax.rem(me + o, devices)
        other = lax.rem(side + q, skies)
        copy = pltpu.make_async_remote_copy(
            src_ref=piece(target),
            dst_ref=got_ref.at[side, me],
            send_sem=send_sem.at[n],
            recv_sem=recv_sem.at[n],
            device_id={"filt": target, "sky": other},
            device_id_type=MESH,
        )
        copy.start()
        copies.append(copy)
    mine.wait()
    for n, (o, q) in enumerate(peers):
        source = lax.rem(me + devices - o, devices)
        other = lax.rem(side + skies - q, skies)
        pltpu.make_async_remote_copy(
            src_ref=piece(me),
            dst_ref=got_ref.at[other, source],
            send_sem=send_sem.at[n],
            recv_sem=recv_sem.at[n],
            device_id={"filt": source, "sky": other},
            device_id_type=MESH,
        ).wait_recv()
    for copy in copies:
        copy.wait_send()


def combine_kernel(dets, temps, first, shift_ref, got_ref, ant_ref, lag_ref, out_ref, a_ref):
    own, width = out_ref.shape[1], out_ref.shape[2]
    skies, devices, count = got_ref.shape[0], got_ref.shape[1], got_ref.shape[2]

    @pl.when(pl.program_id(0) == 0)
    def _():
        for g in range(skies):
            total = got_ref[g, 0].astype(F32)
            for j in range(1, devices):
                total = total + got_ref[g, j].astype(F32)
            line = jnp.concatenate([total[n] for n in range(count)], axis=1)
            if own % LANE or first % LANE:
                line = pltpu.roll(line, shift_ref[0], axis=1)
            tail = 2 * temps * dets
            for k in range(temps):
                norm = line[tail + 2 * k : tail + 2 * k + 1] + line[tail + 2 * k + 1 : tail + 2 * k + 2]
                scale = lax.rsqrt(norm + 1e-06)
                rows = line[2 * dets * k : 2 * dets * (k + 1)] * scale
                rows = rows.astype(BF16).astype(F32)
                for d in range(dets):
                    for c in range(2):
                        row = rows[2 * d + c : 2 * d + c + 1]
                        spread = jnp.broadcast_to(row, (own, count * LANE))
                        turned = pltpu.roll(spread, LANE, axis=1, stride=1, stride_axis=0)
                        a_ref[
                            g * temps + k, c * own : (c + 1) * own, d * LANE : (d + 1) * LANE
                        ] = turned[:, :LANE].astype(BF16)

    slot = lax.broadcasted_iota(jnp.int32, (LANE, width), 0)
    maps = [[], []]
    for d in range(dets):
        hit = slot == (LANE - 1 - DM) - lag_ref[d : d + 1]
        for p in range(2):
            weight = jnp.broadcast_to(ant_ref[p, d : d + 1].astype(F32), (LANE, width))
            maps[p].append(jnp.where(hit, weight, 0.0).astype(BF16))
    maps = [jnp.concatenate(m, axis=0) for m in maps]
    best = None
    for k in range(skies * temps):
        power = None
        for p in range(2):
            r = jnp.dot(a_ref[k], maps[p], preferred_element_type=F32)
            term = r[:own] * r[:own] + r[own:] * r[own:]
            power = term if power is None else power + term
        best = power if best is None else jnp.maximum(best, power)
    out_ref[0] = best


def body(strain, templates, lengths, antenna, delays):
    position = lax.axis_index("filt")
    devices = lax.axis_size("filt")
    skies = lax.axis_size("sky")
    temps = templates.shape[1]
    dets = strain.shape[1]
    bins = strain.shape[2]
    rows = bins // N2
    own = N1 // devices
    first_t = N1 - DM
    count = -(-own // LANE) + 1
    length = count * LANE
    reach = first_t + own * (devices - 1) + length - CENTRE
    half = -(-reach // LANE) * LANE
    blocks = half // LANE
    first = CENTRE + half - first_t - length
    ragged = own % LANE != 0
    got_count = count + 1 if ragged else count

    odd = 2 * np.arange(half) + 1
    b_coarse = host_table(N2 // FINE, FINE, odd, 2 * NF)
    b_fine = host_table(FINE, 1, odd, 2 * NF)
    a_fine = host_table(FINE, 1, odd, 2 * N1)
    turn = 2 * CENTRE - 1
    b_row = (np.arange(N2) * turn) % (2 * NF) * (TWO_PI / (2 * NF))
    pb = jnp.asarray(np.stack([np.cos(b_row), np.sin(b_row)])[:, None, :].astype(np.float32))
    a_ids = position * rows + lax.iota(jnp.int32, rows)
    a_angle = (a_ids * turn % (2 * N1)).astype(F32) * (TWO_PI / (2 * N1))
    pa = jnp.stack([jnp.cos(a_angle), jnp.sin(a_angle)])[:, :, None]
    c_ids = position * rows + FINE * lax.iota(jnp.int32, rows // FINE)
    c_phase = c_ids[:, None] * jnp.asarray(odd, jnp.int32)[None, :] % (2 * N1)
    c_angle = c_phase.astype(F32) * (TWO_PI / (2 * N1))
    a_coarse = jnp.stack([jnp.cos(c_angle), jnp.sin(c_angle)])

    limits = lengths - position * bins
    lines = 2 * temps * dets + 2 * temps

    def whole(shape):
        return pl.BlockSpec(shape, lambda g, *_: (0,) * len(shape))

    def columns(array):
        return pl.BlockSpec(array.shape[:2] + (LANE,), lambda g, *_: (0, 0, g))

    s4 = strain.reshape(2, dets, rows, N2)
    h4 = templates.reshape(2, temps, rows, N2)
    series = pl.pallas_call(
        transform_kernel,
        out_shape=jax.ShapeDtypeStruct((2 * blocks, lines, LANE), BF16),
        grid_spec=pltpu.PrefetchScalarGridSpec(
            num_scalar_prefetch=1,
            grid=(blocks,),
            in_specs=[
                whole(s4.shape),
                whole(h4.shape),
                whole(pa.shape),
                whole(pb.shape),
                columns(b_coarse),
                columns(b_fine),
                columns(a_coarse),
                columns(a_fine),
            ],
            out_specs=whole((2 * blocks, lines, LANE)),
            scratch_shapes=[
                pltpu.VMEM((temps * dets * 2 * rows, N2), BF16),
                pltpu.VMEM((2, lines, LANE), F32),
                pltpu.VMEM((2 * temps, LANE), F32),
            ],
        ),
        compiler_params=pltpu.CompilerParams(dimension_semantics=("arbitrary",)),
        name="transform",
    )(limits, s4, h4, pa, pb, b_coarse, b_fine, a_coarse, a_fine)
    if ragged:
        series = jnp.pad(series, ((0, 1), (0, 0), (0, 0)))

    peers = devices * skies - 1
    got = pl.pallas_call(
        functools.partial(exchange_kernel, devices, skies, first, own),
        out_shape=jax.ShapeDtypeStruct((skies, devices, got_count, lines, LANE), BF16),
        in_specs=[pl.BlockSpec(memory_space=pltpu.VMEM)],
        out_specs=pl.BlockSpec(memory_space=pltpu.VMEM),
        scratch_shapes=[
            pltpu.SemaphoreType.DMA((peers,)),
            pltpu.SemaphoreType.DMA((peers,)),
            pltpu.SemaphoreType.DMA,
        ],
        compiler_params=pltpu.CompilerParams(collective_id=0, has_side_effects=True),
        name="exchange",
    )(series)

    offset = (first - own * position) % LANE
    shift = jnp.reshape((got_count * LANE - offset) % (got_count * LANE), (1,)).astype(jnp.int32)
    if ragged:
        shift = (shift + LANE) % (got_count * LANE)
    sky_local = antenna.shape[2]
    width = 256 if sky_local % 256 == 0 else LANE
    return pl.pallas_call(
        functools.partial(combine_kernel, dets, temps, first),
        out_shape=jax.ShapeDtypeStruct((1, own, sky_local), F32),
        grid_spec=pltpu.PrefetchScalarGridSpec(
            num_scalar_prefetch=1,
            grid=(sky_local // width,),
            in_specs=[
                whole(got.shape),
                pl.BlockSpec((2, dets, width), lambda g, *_: (0, 0, g)),
                pl.BlockSpec((dets, width), lambda g, *_: (0, g)),
            ],
            out_specs=pl.BlockSpec((1, own, width), lambda g, *_: (0, 0, g)),
            scratch_shapes=[pltpu.VMEM((skies * temps, 2 * own, dets * LANE), BF16)],
        ),
        compiler_params=pltpu.CompilerParams(dimension_semantics=("arbitrary",)),
        name="combine",
    )(shift, got, antenna, delays)


def solution(mesh):
    in_specs = (
        P(None, "grp", "filt"),
        P(None, "sky", "filt"),
        P("sky"),
        P(None, None, "sky"),
        P(None, "sky"),
    )
    out_specs = P("grp", "filt", "sky")
    return jax.shard_map(body, mesh=mesh, in_specs=in_specs, out_specs=out_specs, check_vma=False)
```

profile of v0, /device:TPU:0, one launch (start us, length us, event | category | flops | bytes accessed | tf_op | source)
XLA Modules:
  0.0 42.5 jit_solution(11866921558833501218)
XLA Ops:
  0.0 0.9 %fusion.4 = (f32[1,8,1152]{2,1,0:T(8,128)S(1)}, f32[1,8,1152]{2,1,0:T(8,128)S(1)}) fusion(s32[1152]{0:T(1024)} %constant.75.clone, s32[8]{0:T(128)S(1)} %multiply_add_fusion), kind=kLoop, calls=%fused_computation.10 | loop fusion | flops 129024 | bytes 78368 | tf_op jit(solution)/shard_map/cos | solution.py:238
  0.9 0.6 %pad_maximum_fusion.ac_ref = f32[2,8,1152]{2,1,0:T(8,128)} fusion(f32[1,8,1152]{2,1,0:T(8,128)S(1)} %get-tuple-element.6, f32[1,8,1152]{2,1,0:T(8,128)S(1)} %get-tuple-element.5), kind=kLoop, calls=%fused_computation | loop fusion | flops 18432 | bytes 147456 | tf_op jit(solution)/shard_map/stack | solution.py:238
  1.6 0.1 fusion.8
  1.6 0.8 %copy.14.pa_ref = f32[2,128,1]{2,1,0:T(8,128)} copy(f32[2,128,1]{1,0,2:T(2,128)S(1)} %maximum_bitcast_fusion) | data formatting | bytes 2048 | tf_op jit(solution)/shard_map/broadcast_in_dim | solution.py:234
  2.4 1.2 %broadcast_subtract_fusion.limits = s32[2]{0:T(128)} fusion(s32[2]{0:T(128)} %param.12, s32[]{:T(128)S(6)} %mul.89), kind=kLoop, calls=%fused_computation.21 | loop fusion | flops 2 | bytes 20 | tf_op jit(solution)/shard_map/sub | solution.py:240
  3.7 0.0 copy-start
  3.7 2.4 %reshape.199 = bf16[2,3,128,512]{3,2,0,1:T(8,128)(2,1)S(1)} reshape(bf16[2,3,65536]{2,0,1:T(2,128)(2,1)} %param.10) | data formatting | bytes 1572864 | tf_op jit(solution)/shard_map/reshape | solution.py:249
  6.0 0.9 %copy.13.s_ref = bf16[2,3,128,512]{3,2,1,0:T(8,128)(2,1)} copy(bf16[2,3,128,512]{3,2,0,1:T(8,128)(2,1)S(1)} %reshape.199) | data formatting | bytes 1572864 | tf_op jit(solution)/shard_map/reshape | solution.py:249
  7.0 0.0 copy-done
  7.0 0.0 copy-start.1
  7.0 1.1 %reshape.200.h_ref = bf16[2,2,128,512]{3,2,1,0:T(8,128)(2,1)} reshape(bf16[2,2,65536]{2,1,0:T(2,128)(2,1)S(1)} %copy-done) | data formatting | bytes 1048576 | tf_op jit(solution)/shard_map/reshape | solution.py:250
  8.1 10.9 %transform.1.z_ref = bf16[18,16,128]{2,1,0:T(8,128)(2,1)} custom-call(s32[2]{0:T(128)} %broadcast_subtract_fusion.limits, bf16[2,3,128,512]{3,2,1,0:T(8,128)(2,1)} %copy.13.s_ref, bf16[2,2,128,512]{3,2,1,0:T(8,128)(2,1)} %reshape.200.h_ref, f32[2,128,1]{2,1,0:T(8,128)} %copy.14.pa_ref, f32[2,1,512]{2,1,0:T(1,128)} %constant.74.clone.pb_ref, ...), custom_call_target="tpu_custom_call" | custom-call | tf_op jit(solution)/shard_map/transform/pallas_call | solution.py:251
  19.0 12.8 %exchange.1.got_ref = bf16[2,8,3,16,128]{4,3,2,1,0:T(8,128)(2,1)} custom-call(bf16[18,16,128]{2,1,0:T(8,128)(2,1)} %transform.1.z_ref), custom_call_target="tpu_custom_call" | custom-call | tf_op jit(solution)/shard_map/exchange/pallas_call | solution.py:281
  31.8 0.0 copy-done.1
  31.8 0.6 %copy.15.ant_ref = bf16[2,3,1536]{2,1,0:T(4,128)(2,1)} copy(bf16[2,3,1536]{2,0,1:T(2,128)(2,1)S(1)} %copy-done.1) | data formatting | bytes 36864 | tf_op args[3]
  32.4 10.1 %combine.1 = f32[1,256,1536]{2,1,0:T(8,128)} custom-call(s32[1]{0:T(128)} %bitcast.shift_ref, bf16[2,8,3,16,128]{4,3,2,1,0:T(8,128)(2,1)} %exchange.1.got_ref, bf16[2,3,1536]{2,1,0:T(4,128)(2,1)} %copy.15.ant_ref, s32[3,1536]{1,0:T(4,128)} %lag_ref.1), custom_call_target="tpu_custom_call" | custom-call | tf_op jit(solution)/shard_map/combine/pallas_call | solution.py:301
  (2 shorter events, 0.0 us)
Async XLA Ops:
  3.7 3.3 %copy-start = (bf16[2,2,65536]{2,1,0:T(2,128)(2,1)S(1)}, bf16[2,2,65536]{2,1,0:T(2,128)(2,1)}, u32[]{:S(2)}) copy-start(bf16[2,2,65536]{2,1,0:T(2,128)(2,1)} %param.11) | copy-start | bytes 1572868
  7.0 24.8 %copy-start.1 = (bf16[2,3,1536]{2,0,1:T(2,128)(2,1)S(1)}, bf16[2,3,1536]{2,0,1:T(2,128)(2,1)}, u32[]{:S(2)}) copy-start(bf16[2,3,1536]{2,0,1:T(2,128)(2,1)} %param.13) | copy-start | bytes 55300
where the time goes:
time: 43.3 us; the launch traced here: 42.5 us
  Pallas kernels  33.8 us (78%)
  local copies, waits for them, and re-layouts  5.81 us (13%)
  other arithmetic  2.86 us (7%)
    pallas_call x1, Pallas kernels, body(): pl.pallas_call(functools.partial(exchange_kernel, devices, skies, first,...  12.8 us
    pallas_call x1, Pallas kernels, body(): pl.pallas_call(transform_kernel, out_shape=jax.ShapeDtypeStruct((2 * bloc...  10.9 us
    pallas_call x1, Pallas kernels, body(): pl.pallas_call(functools.partial(combine_kernel, dets, temps, first), out...  10.1 us
    reshape x2, local copies, waits for them, and re-layouts, body(): s4 = strain.reshape(2, dets, rows, N2)  3.3 us
    sub x1, other arithmetic, body(): limits = lengths - position * bins  1.23 us
    reshape x1, local copies, waits for them, and re-layouts, body(): h4 = templates.reshape(2, temps, rows, N2)  1.1 us
    cos x1, other arithmetic, body(): a_coarse = jnp.stack([jnp.cos(c_angle), jnp.sin(c_angle)])  0.92 us

commit v1 on v0

v1 whole, which is shorter than its diff:
```python
import functools

import jax
import jax.numpy as jnp
import numpy as np
from jax import lax
from jax.experimental import pallas as pl
from jax.experimental.pallas import tpu as pltpu
from jax.sharding import PartitionSpec as P

N1 = 2048
N2 = 512
DM = 48
NF = N1 * N2
LANE = 128
FINE = 16
TWO_PI = 2.0 * np.pi
CENTRE = N1 - DM + N1 // 2
MESH = pl.DeviceIdType.MESH
F32 = jnp.float32
BF16 = jnp.bfloat16


def host_table(rows, step, columns, period):
    phase = (np.arange(rows)[:, None] * step * columns[None, :]) % period
    angle = phase * (TWO_PI / period)
    return jnp.asarray(np.stack([np.cos(angle), np.sin(angle)]).astype(np.float32))


def outer_turn(coarse, fine):
    c_re, c_im = coarse[0], coarse[1]
    f_re, f_im = fine[0], fine[1]
    re, im = [], []
    for row in range(c_re.shape[0]):
        u, v = c_re[row : row + 1], c_im[row : row + 1]
        re.append(u * f_re - v * f_im)
        im.append(u * f_im + v * f_re)
    return jnp.concatenate(re, axis=0), jnp.concatenate(im, axis=0)


def transform_kernel(
    devices, skies, first, own, lengths, s_ref, h_ref, pa_ref, pb_ref, bc_ref, bf_ref, ac_ref, af_ref, rot_ref,
    out_ref, x_ref, zs_ref, nrm_ref, z_ref, got_ref, send_sem, recv_sem, local_sem,
):
    step = pl.program_id(0)
    blocks = z_ref.shape[0] // 2
    temps, rows = h_ref.shape[1], h_ref.shape[2]
    dets = s_ref.shape[0]
    count = got_ref.shape[2]
    me = lax.axis_index("filt")
    side = lax.axis_index("sky")
    barrier = pltpu.get_barrier_semaphore()
    peers = [(o, q) for q in range(skies) for o in range(devices) if (o, q) != (0, 0)]

    @pl.when(step == 0)
    def _():
        for o, q in peers:
            pl.semaphore_signal(
                barrier,
                inc=1,
                device_id={"filt": lax.rem(me + o, devices), "sky": lax.rem(side + q, skies)},
                device_id_type=MESH,
            )
        p_re, p_im = outer_full(pa_ref, pb_ref)
        ids = lax.broadcasted_iota(jnp.int32, (rows, N2), 0) * N2 + lax.broadcasted_iota(
            jnp.int32, (rows, N2), 1
        )
        for k in range(temps):
            keep = ids < lengths[k] - me * (rows * N2)
            h_re = jnp.where(keep, h_ref[0, k].astype(F32), 0.0)
            h_im = jnp.where(keep, h_ref[1, k].astype(F32), 0.0)
            norm = jnp.sum(h_re * h_re + h_im * h_im, axis=0, keepdims=True)
            norm = jnp.broadcast_to(jnp.sum(norm, axis=1, keepdims=True), (1, LANE))
            high = norm.astype(BF16).astype(F32)
            nrm_ref[2 * k : 2 * k + 1] = high
            nrm_ref[2 * k + 1 : 2 * k + 2] = norm - high
            g_re = h_re * p_re + h_im * p_im
            g_im = h_re * p_im - h_im * p_re
            for d in range(dets):
                s_re = s_ref[d, 0].astype(F32)
                s_im = s_ref[d, 1].astype(F32)
                start = (k * dets + d) * 2 * rows
                x_ref[start : start + rows] = (g_re * s_re - g_im * s_im).astype(BF16)
                x_ref[start + rows : start + 2 * rows] = (g_re * s_im + g_im * s_re).astype(BF16)

    def send(target, q):
        return pltpu.make_async_remote_copy(
            src_ref=z_ref.at[pl.ds((first - own * target) // LANE, count)],
            dst_ref=got_ref.at[side, me],
            send_sem=send_sem.at[target * skies + q],
            recv_sem=recv_sem.at[side * devices + me],
            device_id={"filt": target, "sky": lax.rem(side + q, skies)},
            device_id_type=MESH,
        )

    def keep_own():
        return pltpu.make_async_copy(
            z_ref.at[pl.ds((first - own * me) // LANE, count)], got_ref.at[side, me], local_sem
        )

    def ready(target):
        begin = (first - own * target) // LANE
        last = min(begin + count, 2 * blocks) - 1
        return max(blocks - 1 - begin, last - blocks)

    def send_all(when):
        for target in range(devices):
            if ready(target) == when:
                pl.when(target != me)(lambda target=target: send(target, 0).start())
                pl.when(target == me)(lambda: keep_own().start())
                for q in range(1, skies):
                    send(target, q).start()

    for when in range(blocks - 1):
        if any(ready(target) == when for target in range(devices)):
            @pl.when(step == when + 1)
            def _(when=when):
                if when == min(ready(target) for target in range(devices)):
                    pl.semaphore_wait(barrier, len(peers))
                send_all(when)

    t_re, t_im = outer_turn(bc_ref[...], bf_ref[...])
    table = jnp.concatenate([t_re.astype(BF16), t_im.astype(BF16)], axis=1)
    a_re, a_im = outer_turn(ac_ref[...], af_ref[...])
    up_re, up_im, dn_re, dn_im = [rot_ref[n, pl.ds(me, 1), :] for n in range(4)]
    for item in range(temps * dets):
        start = item * 2 * rows
        r = jnp.dot(x_ref[start : start + 2 * rows], table, preferred_element_type=F32)
        c_re, s_re = r[:rows, :LANE], r[:rows, LANE:]
        c_im, s_im = r[rows:, :LANE], r[rows:, LANE:]
        u_re = jnp.sum(a_re * c_re - a_im * s_re, axis=0, keepdims=True)
        u_im = jnp.sum(a_re * c_im - a_im * s_im, axis=0, keepdims=True)
        v_re = jnp.sum(a_re * s_re + a_im * c_re, axis=0, keepdims=True)
        v_im = jnp.sum(a_re * s_im + a_im * c_im, axis=0, keepdims=True)
        p_re, p_im = u_re - v_im, u_im + v_re
        m_re, m_im = u_re + v_im, u_im - v_re
        zs_ref[0, 2 * item : 2 * item + 1] = p_re * up_re - p_im * up_im
        zs_ref[0, 2 * item + 1 : 2 * item + 2] = p_re * up_im + p_im * up_re
        zs_ref[1, 2 * item : 2 * item + 1] = m_re * dn_re - m_im * dn_im
        zs_ref[1, 2 * item + 1 : 2 * item + 2] = m_re * dn_im + m_im * dn_re
    tail = 2 * temps * dets
    zs_ref[0, tail : tail + 2 * temps] = nrm_ref[...]
    zs_ref[1, tail : tail + 2 * temps] = nrm_ref[...]
    flip = (
        lax.broadcasted_iota(jnp.int32, (LANE, LANE), 0)
        + lax.broadcasted_iota(jnp.int32, (LANE, LANE), 1)
        == LANE - 1
    )
    flip = jnp.where(flip, 1.0, 0.0).astype(BF16)
    ahead = jnp.dot(zs_ref[0].astype(BF16), flip, preferred_element_type=F32)
    z_ref[blocks - 1 - step] = ahead.astype(BF16)
    z_ref[blocks + step] = zs_ref[1].astype(BF16)

    @pl.when(step == blocks - 1)
    def _():
        send_all(blocks - 1)
        keep_own().wait()
        for q in range(skies):
            for source in range(devices):
                def arrive(source=source, q=q):
                    other = lax.rem(side + q, skies)
                    pltpu.make_async_remote_copy(
                        src_ref=z_ref.at[pl.ds(0, count)],
                        dst_ref=got_ref.at[other, source],
                        send_sem=send_sem.at[source * skies + q],
                        recv_sem=recv_sem.at[other * devices + source],
                        device_id={"filt": source, "sky": other},
                        device_id_type=MESH,
                    ).wait_recv()
                if q:
                    arrive()
                else:
                    pl.when(source != me)(arrive)
        for g in range(skies):
            total = got_ref[g, 0].astype(F32)
            for j in range(1, devices):
                total = total + got_ref[g, j].astype(F32)
            out_ref[g] = total
        for target in range(devices):
            pl.when(target != me)(lambda target=target: send(target, 0).wait_send())
            for q in range(1, skies):
                send(target, q).wait_send()


def outer_full(pa_ref, pb_ref):
    rows = pa_ref.shape[1]
    a_re = jnp.concatenate([pa_ref[0]] * (N2 // LANE), axis=1)
    a_im = jnp.concatenate([pa_ref[1]] * (N2 // LANE), axis=1)
    b_re, b_im = pb_ref[0], pb_ref[1]
    return a_re * b_re - a_im * b_im, a_re * b_im + a_im * b_re


def combine_kernel(dets, temps, first, shift_ref, got_ref, ant_ref, lag_ref, out_ref, a_ref):
    own, width = out_ref.shape[1], out_ref.shape[2]
    skies, count = got_ref.shape[0], got_ref.shape[1]

    @pl.when(pl.program_id(0) == 0)
    def _():
        for g in range(skies):
            line = jnp.concatenate([got_ref[g, n] for n in range(count)], axis=1)
            if own % LANE or first % LANE:
                line = pltpu.roll(line, shift_ref[0], axis=1)
            tail = 2 * temps * dets
            for k in range(temps):
                norm = line[tail + 2 * k : tail + 2 * k + 1] + line[tail + 2 * k + 1 : tail + 2 * k + 2]
                scale = lax.rsqrt(norm + 1e-06)
                rows = line[2 * dets * k : 2 * dets * (k + 1)] * scale
                rows = rows.astype(BF16).astype(F32)
                for d in range(dets):
                    for c in range(2):
                        row = rows[2 * d + c : 2 * d + c + 1]
                        spread = jnp.broadcast_to(row, (own, count * LANE))
                        turned = pltpu.roll(spread, LANE, axis=1, stride=1, stride_axis=0)
                        a_ref[
                            g * temps + k, c * own : (c + 1) * own, d * LANE : (d + 1) * LANE
                        ] = turned[:, :LANE].astype(BF16)

    slot = lax.broadcasted_iota(jnp.int32, (LANE, width), 0)
    maps = [[], []]
    for d in range(dets):
        hit = slot == (LANE - 1 - DM) - lag_ref[d : d + 1]
        for p in range(2):
            weight = jnp.broadcast_to(ant_ref[d, p : p + 1].astype(F32), (LANE, width))
            maps[p].append(jnp.where(hit, weight, 0.0).astype(BF16))
    maps = [jnp.concatenate(m, axis=0) for m in maps]
    best = None
    for k in range(skies * temps):
        power = None
        for p in range(2):
            r = jnp.dot(a_ref[k], maps[p], preferred_element_type=F32)
            term = r[:own] * r[:own] + r[own:] * r[own:]
            power = term if power is None else power + term
        best = power if best is None else jnp.maximum(best, power)
    out_ref[0] = best


def body(strain, templates, lengths, antenna, delays):
    position = lax.axis_index("filt")
    devices = lax.axis_size("filt")
    skies = lax.axis_size("sky")
    temps = templates.shape[1]
    dets = strain.shape[1]
    bins = strain.shape[2]
    rows = bins // N2
    own = N1 // devices
    first_t = N1 - DM
    count = -(-own // LANE) + 1
    length = count * LANE
    reach = first_t + own * (devices - 1) + length - CENTRE
    half = -(-reach // LANE) * LANE
    blocks = half // LANE
    first = CENTRE + half - first_t - length
    ragged = own % LANE != 0
    got_count = count + 1 if ragged else count

    odd = 2 * np.arange(half) + 1
    b_coarse = host_table(N2 // FINE, FINE, odd, 2 * NF)
    b_fine = host_table(FINE, 1, odd, 2 * NF)
    a_fine = host_table(FINE, 1, odd, 2 * N1)
    turn = 2 * CENTRE - 1
    b_row = (np.arange(N2) * turn) % (2 * NF) * (TWO_PI / (2 * NF))
    pb = jnp.asarray(np.stack([np.cos(b_row), np.sin(b_row)])[:, None, :].astype(np.float32))
    pa = host_table(rows, turn, np.ones(LANE, np.int64), 2 * N1)
    a_coarse = host_table(rows // FINE, FINE, odd, 2 * N1)
    shifts = np.arange(devices)[:, None] * rows
    rot = []
    for sign in (1, -1):
        angle = shifts * (turn + sign * odd[None, :]) % (2 * N1) * (TWO_PI / (2 * N1))
        rot += [np.cos(angle), np.sin(angle)]
    rot = jnp.asarray(np.stack(rot).astype(np.float32))

    lines = 2 * temps * dets + 2 * temps

    def whole(shape):
        return pl.BlockSpec(shape, lambda g, *_: (0,) * len(shape))

    def columns(array):
        return pl.BlockSpec(array.shape[:2] + (LANE,), lambda g, *_: (0, 0, g))

    s4 = strain.transpose(1, 0, 2).reshape(dets, 2, rows, N2)
    h4 = templates.reshape(2, temps, rows, N2)
    peers = devices * skies
    got = pl.pallas_call(
        functools.partial(transform_kernel, devices, skies, first, own),
        out_shape=jax.ShapeDtypeStruct((skies, got_count, lines, LANE), F32),
        grid_spec=pltpu.PrefetchScalarGridSpec(
            num_scalar_prefetch=1,
            grid=(blocks,),
            in_specs=[
                whole(s4.shape),
                whole(h4.shape),
                whole(pa.shape),
                whole(pb.shape),
                columns(b_coarse),
                columns(b_fine),
                columns(a_coarse),
                columns(a_fine),
                columns(rot),
            ],
            out_specs=whole((skies, got_count, lines, LANE)),
            scratch_shapes=[
                pltpu.VMEM((temps * dets * 2 * rows, N2), BF16),
                pltpu.VMEM((2, lines, LANE), F32),
                pltpu.VMEM((2 * temps, LANE), F32),
                pltpu.VMEM((2 * blocks, lines, LANE), BF16),
                pltpu.VMEM((skies, devices, got_count, lines, LANE), BF16),
                pltpu.SemaphoreType.DMA((peers,)),
                pltpu.SemaphoreType.DMA((peers,)),
                pltpu.SemaphoreType.DMA,
            ],
        ),
        compiler_params=pltpu.CompilerParams(
            dimension_semantics=("arbitrary",), collective_id=0, has_side_effects=True
        ),
        name="transform",
    )(lengths, s4, h4, pa, pb, b_coarse, b_fine, a_coarse, a_fine, rot)

    offset = (first - own * position) % LANE
    shift = jnp.reshape((got_count * LANE - offset) % (got_count * LANE), (1,)).astype(jnp.int32)
    if ragged:
        shift = (shift + LANE) % (got_count * LANE)
    sky_local = antenna.shape[2]
    width = 256 if sky_local % 256 == 0 else LANE
    return pl.pallas_call(
        functools.partial(combine_kernel, dets, temps, first),
        out_shape=jax.ShapeDtypeStruct((1, own, sky_local), F32),
        grid_spec=pltpu.PrefetchScalarGridSpec(
            num_scalar_prefetch=1,
            grid=(sky_local // width,),
            in_specs=[
                whole(got.shape),
                pl.BlockSpec((dets, 2, width), lambda g, *_: (0, 0, g)),
                pl.BlockSpec((dets, width), lambda g, *_: (0, g)),
            ],
            out_specs=pl.BlockSpec((1, own, width), lambda g, *_: (0, 0, g)),
            scratch_shapes=[pltpu.VMEM((skies * temps, 2 * own, dets * LANE), BF16)],
        ),
        compiler_params=pltpu.CompilerParams(dimension_semantics=("arbitrary",)),
        name="combine",
    )(shift, got, antenna.transpose(1, 0, 2), delays)


def solution(mesh):
    in_specs = (
        P(None, "grp", "filt"),
        P(None, "sky", "filt"),
        P("sky"),
        P(None, None, "sky"),
        P(None, "sky"),
    )
    out_specs = P("grp", "filt", "sky")
    return jax.shard_map(body, mesh=mesh, in_specs=in_specs, out_specs=out_specs, check_vma=False)
```

time: 43.3 us -> 33.1 us (0.76)
  Pallas kernels: 33.8 us -> 28.5 us
  other arithmetic: 2.86 us -> 0 us
  local copies, waits for them, and re-layouts: 5.81 us -> 3.94 us
    pallas_call x2 -> x1, Pallas kernels: 23.7 us -> 18.4 us  [body(): pl.pallas_call(functools.partial(transform_kernel, devices, skies, first,...]
    reshape x2 -> x1, local copies, waits for them, and re-layouts: 3.3 us -> 1.81 us  [body(): s4 = strain.transpose(1, 0, 2).reshape(dets, 2, rows, N2)]
    sub x1 -> x0, other arithmetic: 1.23 us -> none  [body(): limits = lengths - position * bins]
    reshape x1, local copies, waits for them, and re-layouts: 1.1 us -> 2.13 us  [body(): h4 = templates.reshape(2, temps, rows, N2)]
    cos x1 -> x0, other arithmetic: 0.92 us -> none  [body(): a_coarse = jnp.stack([jnp.cos(c_angle), jnp.sin(c_angle)])]
    broadcast_in_dim x1 -> x0, local copies, waits for them, and re-layouts: 0.79 us -> none  [body(): pa = jnp.stack([jnp.cos(a_angle), jnp.sin(a_angle)])[:, :, None]]
    another operation x1 -> x0, other arithmetic: 0.64 us -> none  [body(): a_coarse = jnp.stack([jnp.cos(c_angle), jnp.sin(c_angle)])]
    unnamed x5 -> x2, local copies, waits for them, and re-layouts: 0.62 us -> 0.01 us
where the time goes in v1:
time: 33.1 us; the launch traced here: 32.4 us
  Pallas kernels  28.5 us (86%)
  local copies, waits for them, and re-layouts  3.94 us (12%)
    pallas_call x1, Pallas kernels, body(): pl.pallas_call(functools.partial(transform_kernel, devices, skies, first,...  18.4 us
    pallas_call x1, Pallas kernels, body(): pl.pallas_call(functools.partial(combine_kernel, dets, temps, first), out...  10 us
    reshape x1, local copies, waits for them, and re-layouts, body(): h4 = templates.reshape(2, temps, rows, N2)  2.13 us
    reshape x1, local copies, waits for them, and re-layouts, body(): s4 = strain.transpose(1, 0, 2).reshape(dets, 2, rows, N2)  1.81 us

profile of v1, /device:TPU:0, one launch (start us, length us, event | category | flops | bytes accessed | tf_op | source)
XLA Modules:
  0.0 32.4 jit_solution(8628887484882423850)
XLA Ops:
  0.0 0.0 copy-start
  0.0 2.1 %reshape.11.h_ref = bf16[2,2,128,512]{3,2,1,0:T(8,128)(2,1)} reshape(bf16[2,2,65536]{2,1,0:T(2,128)(2,1)} %param.13) | data formatting | bytes 1048576 | tf_op jit(solution)/shard_map/reshape | solution.py:281
  2.1 0.0 copy-done
  2.1 1.8 %reshape.10.s_ref = bf16[3,2,128,512]{3,2,1,0:T(8,128)(2,1)} reshape(bf16[3,2,65536]{2,1,0:T(2,128)(2,1)S(1)} %bitcast.3) | data formatting | bytes 1572864 | tf_op jit(solution)/shard_map/reshape | solution.py:280
  3.9 18.4 %transform.1.got_ref = f32[2,3,16,128]{3,2,1,0:T(8,128)} custom-call(s32[2]{0:T(128)} %lengths.1, bf16[3,2,128,512]{3,2,1,0:T(8,128)(2,1)} %reshape.10.s_ref, bf16[2,2,128,512]{3,2,1,0:T(8,128)(2,1)} %reshape.11.h_ref, f32[2,128,128]{2,1,0:T(8,128)} %constant.48.clone.pa_ref, f32[2,1,512]{2,1,0:T(1,128)} %constant.47.clone.pb_ref, ...), custom_call_target="tpu_custom_call" | custom-call | tf_op jit(solution)/shard_map/transform/pallas_call | solution.py:283
  22.4 10.0 %combine.1 = f32[1,256,1536]{2,1,0:T(8,128)} custom-call(s32[1]{0:T(128)} %bitcast.shift_ref, f32[2,3,16,128]{3,2,1,0:T(8,128)} %transform.1.got_ref, bf16[3,2,1536]{2,1,0:T(2,128)(2,1)} %bitcast.4, s32[3,1536]{1,0:T(4,128)} %lag_ref.1), custom_call_target="tpu_custom_call" | custom-call | tf_op jit(solution)/shard_map/combine/pallas_call | solution.py:324
Async XLA Ops:
  0.0 2.1 %copy-start = (bf16[2,3,65536]{2,0,1:T(2,128)(2,1)S(1)}, bf16[2,3,65536]{2,0,1:T(2,128)(2,1)}, u32[]{:S(2)}) copy-start(bf16[2,3,65536]{2,0,1:T(2,128)(2,1)} %param.12) | copy-start | bytes 2359300
